TPU v7x, 512 devices: a whole 4x4x16 slice. The times are simulated.
512 devices in a mesh: slab: 128 (over y, z, core), tile: 4 (over x).
Axes of the slice: x: 4, y: 4, z: 16, core: 2. Of those that a mesh axis runs over, the one named last changes fastest.
Arguments:
- tokens: bfloat16 [1024, 1024, 128], P('slab', 'tile'), may hold values from -6 to 6
- conv_weight: float32 [3, 3, 128], replicated, may hold values from -2.5 to 2.5
- occupancy: int32 [16, 16], replicated, may hold values 0 or 1
- row_gain: float32 [128], replicated, may hold values from 0.1 to 1.9
- row_qkv: bfloat16 [128, 384], replicated, may hold values from -5 to 5
- row_out: bfloat16 [128, 128], replicated, may hold values from -0.5 to 0.5
- col_gain: float32 [128], replicated, may hold values from 0.1 to 1.9
- col_qkv: bfloat16 [128, 384], replicated, may hold values from -5 to 5
- col_out: bfloat16 [128, 128], replicated, may hold values from -0.5 to 0.5
Outputs:
- mixed: bfloat16 [1024, 1024, 128], P(None, ('tile', 'slab'))
All inputs are finite; a program needn't handle non-finite values.
Results may differ from a plain program's by a relative error of at most 0.02.
Values may be sent and summed in bfloat16 or wider, within the bound.
A program may use at most 64 MiB of HBM per device.

v0:
```python
import math
import jax
import jax.numpy as jnp
from jax import lax
from jax.sharding import PartitionSpec as P

HEAD_DIM = 32
COL_REACH = 128


def padded_2(block, sides, width):
    for axis, dim in sides:
        count = lax.axis_size(axis)
        forward = [(i, i + 1) for i in range(count - 1)]
        backward = [(target, source) for source, target in forward]
        low = lax.ppermute(
            lax.slice_in_dim(block, block.shape[dim] - width, None, axis=dim), axis, forward
        )
        high = lax.ppermute(lax.slice_in_dim(block, 0, width, axis=dim), axis, backward)
        block = jnp.concatenate([low, block, high], axis=dim)
    return block


def attend(queries, key_block, value_block, query_pos, key_pos, query_ok, key_ok, band_reach):
    query_count = queries.shape[0]
    key_count = key_block.shape[0]
    head_count = queries.shape[1] // HEAD_DIM
    query_heads = queries.reshape(query_count, head_count, HEAD_DIM)
    key_heads = key_block.reshape(key_count, head_count, HEAD_DIM)
    value_heads = value_block.reshape(key_count, head_count, HEAD_DIM)
    scores = jnp.einsum(
        "qhd,khd->hqk", query_heads, key_heads, preferred_element_type=jnp.float32
    ) / math.sqrt(HEAD_DIM)
    offsets = query_pos[:, None] - key_pos[None, :]
    allowed = (jnp.abs(offsets) < band_reach) & ((key_ok[None, :] > 0) | (offsets == 0))
    scores = jnp.where(allowed[None], scores, jnp.float32(-1e30))
    row_max = jnp.max(scores, axis=-1, keepdims=True)
    exp_terms = jnp.exp(scores - row_max)
    row_total = jnp.sum(exp_terms, axis=-1, keepdims=True)
    weights = (exp_terms / row_total).astype(jnp.bfloat16)
    mixture = jnp.einsum("hqk,khd->qhd", weights, value_heads, preferred_element_type=jnp.float32)
    mixture = mixture * query_ok[:, None, None].astype(jnp.float32)
    return mixture.reshape(query_count, head_count * HEAD_DIM).astype(jnp.bfloat16)


def attend_line(projected, line_ok, band_reach):
    line_len = projected.shape[0]
    model_width = projected.shape[1] // 3
    block_rows = min(256, line_len)
    block_count = line_len // block_rows
    queries = projected[:, :model_width]
    key_value = jnp.pad(projected[:, model_width:], ((band_reach, band_reach), (0, 0)))
    padded_ok = jnp.pad(line_ok, (band_reach, band_reach))
    positions = jnp.arange(line_len + 2 * band_reach, dtype=jnp.int32) - band_reach

    def one_block(block_index):
        block_start = block_index * block_rows
        query_part = lax.dynamic_slice_in_dim(queries, block_start, block_rows, 0)
        query_ok = lax.dynamic_slice_in_dim(line_ok, block_start, block_rows, 0)
        query_pos = lax.dynamic_slice_in_dim(positions, block_start + band_reach, block_rows, 0)
        kv_part = lax.dynamic_slice_in_dim(key_value, block_start, block_rows + 2 * band_reach, 0)
        key_ok = lax.dynamic_slice_in_dim(padded_ok, block_start, block_rows + 2 * band_reach, 0)
        key_pos = lax.dynamic_slice_in_dim(positions, block_start, block_rows + 2 * band_reach, 0)
        return attend(
            query_part,
            kv_part[:, :model_width],
            kv_part[:, model_width:],
            query_pos,
            key_pos,
            query_ok,
            key_ok,
            band_reach,
        )

    blocks = lax.map(one_block, jnp.arange(block_count, dtype=jnp.int32))
    return blocks.reshape(line_len, model_width)


def layer_norm(stream, gain):
    values32 = stream.astype(jnp.float32)
    center = jnp.mean(values32, axis=-1, keepdims=True)
    centered = values32 - center
    spread = jnp.mean(centered * centered, axis=-1, keepdims=True)
    return (centered * lax.rsqrt(spread + 1e-05) * gain).astype(jnp.bfloat16)


def column_part(stream, col_ok, gain, qkv_weight, out_weight):
    normed = layer_norm(stream, gain)
    projected = jnp.dot(normed, qkv_weight, preferred_element_type=jnp.float32).astype(jnp.bfloat16)
    by_column = jnp.moveaxis(projected, 1, 0)
    ok_column = jnp.moveaxis(col_ok, 1, 0)
    mixture = lax.map(
        lambda pieces: attend_line(pieces[0], pieces[1], COL_REACH), (by_column, ok_column)
    )
    mixture = jnp.moveaxis(mixture, 0, 1)
    update = jnp.dot(mixture, out_weight, preferred_element_type=jnp.float32)
    return (stream.astype(jnp.float32) + update).astype(jnp.bfloat16)


def local(tokens, conv_weight, occupancy, row_gain, row_qkv, row_out, col_gain, col_qkv, col_out):
    row_count, length, model_width = tokens.shape
    slab_count = lax.axis_size("slab")
    slab_at = lax.axis_index("slab")
    tile_at = lax.axis_index("tile")
    height = row_count * slab_count
    block_size = height // occupancy.shape[0]
    band_reach = min(128, length)
    col_count = length // slab_count
    padded = padded_2(tokens, (("slab", 0), ("tile", 1)), 1)
    padded32 = padded.astype(jnp.float32)
    convolved = padded32[1 : 1 + row_count, 1 : 1 + length]
    for shift_row in range(3):
        for shift_col in range(3):
            convolved = (
                convolved
                + conv_weight[shift_row, shift_col]
                * padded32[shift_row : shift_row + row_count, shift_col : shift_col + length]
            )
    stream = convolved.astype(jnp.bfloat16)
    normed = layer_norm(stream, row_gain)
    projected = jnp.dot(normed, row_qkv, preferred_element_type=jnp.float32).astype(jnp.bfloat16)
    queries = projected[..., :model_width]
    line_ids = (slab_at * row_count + jnp.arange(row_count, dtype=jnp.int32)) // block_size
    selector = (
        line_ids[:, None] == jnp.arange(occupancy.shape[0], dtype=jnp.int32)[None, :]
    ).astype(jnp.int32)
    occ_rows = jnp.dot(selector, occupancy)
    occ_line = jnp.repeat(occ_rows, block_size, axis=1)
    occ_wide = jnp.pad(occ_line, ((0, 0), (band_reach, band_reach)))
    key_ok = lax.dynamic_slice_in_dim(occ_wide, tile_at * length, length + 2 * band_reach, 1)
    query_ok = key_ok[:, band_reach : band_reach + length]
    kv_wide = padded_2(projected[..., model_width:], (("tile", 1),), band_reach)
    query_pos = tile_at * length + jnp.arange(length, dtype=jnp.int32)
    key_pos = tile_at * length - band_reach + jnp.arange(length + 2 * band_reach, dtype=jnp.int32)

    def row_attend(pieces):
        query_row, kv_row, qok_row, kok_row = pieces
        return attend(
            query_row,
            kv_row[:, :model_width],
            kv_row[:, model_width:],
            query_pos,
            key_pos,
            qok_row,
            kok_row,
            band_reach,
        )

    mixture = lax.map(row_attend, (queries, kv_wide, query_ok, key_ok))
    after_rows = (
        stream.astype(jnp.float32) + jnp.dot(mixture, row_out, preferred_element_type=jnp.float32)
    ).astype(jnp.bfloat16)
    columns = lax.all_to_all(after_rows, "slab", split_axis=1, concat_axis=0, tiled=True)
    col_ids = (
        tile_at * length + slab_at * col_count + jnp.arange(col_count, dtype=jnp.int32)
    ) // block_size
    col_selector = (
        jnp.arange(occupancy.shape[1], dtype=jnp.int32)[:, None] == col_ids[None, :]
    ).astype(jnp.int32)
    occ_blocks = jnp.dot(occupancy, col_selector)
    col_ok = jnp.repeat(occ_blocks, block_size, axis=0)
    result = column_part(columns, col_ok, col_gain, col_qkv, col_out)
    return result


def solution(mesh):
    return jax.shard_map(
        local,
        mesh=mesh,
        in_specs=(P("slab", "tile", None), P(), P(), P(), P(), P(), P(), P(), P()),
        out_specs=P(None, ("tile", "slab"), None),
        check_vma=False,
    )
```

profile of v0, /device:TPU:1, one launch (start us, length us, event | category | flops | bytes accessed | tf_op | source)
XLA Modules:
  0.0 189.0 jit_solution(11534198888149711325)
XLA Ops:
  0.9 4.9 %collective-permute-start = (bf16[1,256,128]{2,1,0:T(8,128)(2,1)S(1)}, bf16[1,256,128]{2,1,0:T(8,128)(2,1)S(1)}, u32[]{:S(2)}, u32[]{:S(2)}) collective-permute-start(bf16[1,256,128]{2,1,0:T(8,128)(2,1)S(1)} %get-tuple-element.356), channel_id=1, source_target_pairs={{0,4},{4,8},{8,12},{12,16},{16,20},{20,24},{24,28},{28,32},{32,36}... | collective-permute-start | bytes 196616 | tf_op jit(solution)/shard_map/ppermute | solution.py:16
  5.9 5.1 %collective-permute-start.1 = (bf16[1,256,128]{2,1,0:T(8,128)(2,1)S(1)}, bf16[1,256,128]{2,1,0:T(8,128)(2,1)S(1)}, u32[]{:S(2)}, u32[]{:S(2)}) collective-permute-start(bf16[1,256,128]{2,1,0:T(8,128)(2,1)S(1)} %get-tuple-element.355), channel_id=1, source_target_pairs={{4,0},{8,4},{12,8},{16,12},{20,16},{24,20},{28,24},{32,28},{36,32}... | collective-permute-start | bytes 196616 | tf_op jit(solution)/shard_map/ppermute | solution.py:19
  11.0 1.1 constant_dynamic-update-slice_fusion.3
  12.2 2.4 %collective-permute-start.2 = (bf16[10,1,128]{2,1,0:T(2,128)(2,1)S(1)}, bf16[10,1,128]{2,1,0:T(2,128)(2,1)S(1)}, u32[]{:S(2)}, u32[]{:S(2)}) collective-permute-start(bf16[10,1,128]{2,1,0:T(2,128)(2,1)S(1)} %get-tuple-element.353), channel_id=1, source_target_pairs={{0,1},{1,2},{2,3},{4,5},{5,6},{6,7},{8,9},{9,10},{10,11},{12,13},{... | collective-permute-start | bytes 7688 | tf_op jit(solution)/shard_map/ppermute | solution.py:16
  14.6 1.3 collective-permute-start.3
  16.8 2.2 %collective-permute-done.3 = bf16[10,1,128]{2,1,0:T(2,128)(2,1)S(1)} collective-permute-done((bf16[10,1,128]{2,1,0:T(2,128)(2,1)S(1)}, bf16[10,1,128]{2,1,0:T(2,128)(2,1)S(1)}, u32[]{:S(2)}, u32[]{:S(2)}) %collective-permute-start.3) | collective-permute-done | bytes 2592 | tf_op jit(solution)/shard_map/ppermute | solution.py:19
  19.1 1.2 convert_reduce_fusion
  21.0 1.0 convolution_convert_fusion.1
  22.1 1.0 fusion.83
  23.0 3.9 %collective-permute-start.4 = (bf16[8,128,256]{2,1,0:T(8,128)(2,1)}, bf16[8,128,256]{2,1,0:T(8,128)(2,1)}, u32[]{:S(2)}, u32[]{:S(2)}) collective-permute-start(bf16[8,128,256]{2,1,0:T(8,128)(2,1)} %get-tuple-element.351), channel_id=1, source_target_pairs={{0,1},{1,2},{2,3},{4,5},{5,6},{6,7},{8,9},{9,10},{10,11},{12,13},{... | collective-permute-start | bytes 1572872 | tf_op jit(solution)/shard_map/ppermute | solution.py:16
  26.9 1.3 collective-permute-start.5
  28.8 8.9 %collective-permute-done.4 = bf16[8,128,256]{2,1,0:T(8,128)(2,1)} collective-permute-done((bf16[8,128,256]{2,1,0:T(8,128)(2,1)}, bf16[8,128,256]{2,1,0:T(8,128)(2,1)}, u32[]{:S(2)}, u32[]{:S(2)}) %collective-permute-start.4) | collective-permute-done | bytes 524320 | tf_op jit(solution)/shard_map/ppermute | solution.py:16
  37.7 4.7 %collective-permute-done.5 = bf16[8,128,256]{2,1,0:T(8,128)(2,1)} collective-permute-done((bf16[8,128,256]{2,1,0:T(8,128)(2,1)S(1)}, bf16[8,128,256]{2,1,0:T(8,128)(2,1)}, u32[]{:S(2)}, u32[]{:S(2)}) %collective-permute-start.5) | collective-permute-done | bytes 524320 | tf_op jit(solution)/shard_map/ppermute | solution.py:19
  42.4 2.7 %pad_maximum_fusion = bf16[8,512,256]{2,1,0:T(8,128)(2,1)} fusion(bf16[8,128,256]{2,1,0:T(8,128)(2,1)} %collective-permute-done.5, bf16[8,256,256]{2,1,0:T(8,128)(2,1)S(1)} %slice.161, bf16[8,128,256]{2,1,0:T(8,128)(2,1)} %collective-permute-done.4), kind=kLoop, calls=%fused_computation.61 | loop fusion | flops 6291456 | bytes 4194304 | tf_op jit(solution)/shard_map/concatenate | solution.py:20
  45.1 29.7 %while.45 = (s32[]{:T(128)}, bf16[8,256,128]{1,2,0:T(8,128)(2,1)S(1)}, bf16[8,512,256]{2,1,0:T(8,128)(2,1)}, s32[8,512]{1,0:T(8,128)S(1)}, bf16[8,256,128]{2,1,0...) while((s32[]{:T(128)}, bf16[8,256,128]{1,2,0:T(8,128)(2,1)S(1)}, ...), condition=%wide.region_5.6_spmd.clone, body=%wide.region_2.5_spmd.clone.sunk | while | flops 106237440 | bytes 2969721 | solution.py:149
  45.4 1.0 constant_dynamic-slice_fusion.15
  46.7 1.0 fusion.124
  47.7 1.1 fusion.126
  49.1 1.0 constant_dynamic-slice_fusion.15
  50.4 1.0 fusion.124
  51.4 1.1 fusion.126
  52.8 1.0 constant_dynamic-slice_fusion.15
  54.1 1.0 fusion.124
  55.1 1.1 fusion.126
  56.5 1.0 constant_dynamic-slice_fusion.15
  58.8 1.1 fusion.126
  60.2 1.0 constant_dynamic-slice_fusion.15
  62.5 1.1 fusion.126
  64.0 1.0 constant_dynamic-slice_fusion.15
  65.2 1.0 fusion.124
  66.2 1.1 fusion.126
  67.7 1.0 constant_dynamic-slice_fusion.15
  69.0 1.0 fusion.124
  69.9 1.1 fusion.126
  71.4 1.0 constant_dynamic-slice_fusion.15
  72.7 1.0 fusion.124
  73.7 1.1 fusion.126
  75.1 1.1 copy.40
  76.3 19.1 %all-to-all-start = ((bf16[8,256,128]{2,0,1:T(8,128)(2,1)}), bf16[8,256,128]{2,0,1:T(8,128)(2,1)S(1)}, u32[]{:S(2)}, u32[]{:S(2)}) async-start(bf16[8,256,128]{2,0,1:T(8,128)(2,1)} %copy.40), calls=%async_computation | async-start | bytes 1048576 | tf_op jit(solution)/shard_map/all_to_all | solution.py:153
  95.7 32.8 %all-to-all-done = bf16[8,256,128]{2,0,1:T(8,128)(2,1)S(1)} async-done(((bf16[8,256,128]{2,0,1:T(8,128)(2,1)}), bf16[8,256,128]{2,0,1:T(8,128)(2,1)S(1)}, u32[]{:S(2)}, u32[]{:S(2)}) %all-to-all-start) | async-done | bytes 524320 | tf_op jit(solution)/shard_map/all_to_all | solution.py:153
  128.6 1.1 fusion.78
  129.8 1.5 copy.65
  131.9 14.7 %multiply_reduce_fusion = f32[128,8,2]{2,0,1:T(8,128)S(1)} fusion(f32[128,8,2]{2,0,1:T(8,128)S(1)} %copy.45, f32[8,128,2,128]{3,0,2,1:T(8,128)S(1)} %bitcast_convert_fusion), kind=kLoop, calls=%fused_computation.100 | loop fusion | flops 784384 | bytes 1064960 | tf_op jit(solution)/shard_map/reduce_sum | solution.py:83
  147.2 2.2 %fusion.41 = bf16[2,1024,384]{2,1,0:T(8,128)(2,1)S(1)} fusion(f32[128,8,2,128]{3,2,0,1:T(2,128)} %bitcast.154, f32[128]{0:T(128)S(1)} %copy-done.7, f32[1024,2]{0,1:T(2,128)S(1)} %rsqrt.21, f32[1024,2]{0,1:T(2,128)S(1)} %div.73, bf16[128,384]{1,0:T(8,128)(2,1)S(1)} %copy-done.2), kind=kOutput, calls=%fused_computation.67 | convolution fusion | flops 203161600 | bytes 2736640 | tf_op jit(solution)/shard_map/dot_general | solution.py:89
  149.4 36.1 %while.44 = (s32[]{:T(128)}, bf16[2,1024,128]{2,1,0:T(8,128)(2,1)}, bf16[2,1024,384]{2,1,0:T(8,128)(2,1)S(1)}, s32[2,1024]{1,0:T(2,128)S(1)}, s32[]{:T(128)}, /*...) while((s32[]{:T(128)}, bf16[2,1024,128]{2,1,0:T(8,128)(2,1)}, ...), condition=%wide.region_13.14_spmd, body=%wide.region_8.13_spmd.sunk | while | flops 106237968 | bytes 8370293 | solution.py:92
  150.0 16.7 %while.46 = (s32[]{:T(128)}, bf16[4,256,128]{2,1,0:T(8,128)(2,1)S(1)}, s32[4]{0:T(128)S(1)}, bf16[1280,256]{0,1:T(8,128)(2,1)S(1)}, s32[1280]{0:T(1024)S(1)}, /*...) while((s32[]{:T(128)}, ...), condition=%wide.region_12.12_spmd.clone, body=%wide.region_9.11_spmd.clone.sunk | while | flops 106236688 | bytes 1924418 | solution.py:75
  152.9 1.1 fusion.134
  156.1 1.0 fusion.133
  157.1 1.1 fusion.134
  160.3 1.0 fusion.133
  161.3 1.1 fusion.134
  164.4 1.0 fusion.133
  165.5 1.1 fusion.134
  168.1 16.7 %while.46 = (s32[]{:T(128)}, bf16[4,256,128]{2,1,0:T(8,128)(2,1)S(1)}, s32[4]{0:T(128)S(1)}, bf16[1280,256]{0,1:T(8,128)(2,1)S(1)}, s32[1280]{0:T(1024)S(1)}, /*...) while((s32[]{:T(128)}, ...), condition=%wide.region_12.12_spmd.clone, body=%wide.region_9.11_spmd.clone.sunk | while | flops 106236688 | bytes 1924418 | solution.py:75
  170.0 1.0 fusion.133
  171.0 1.1 fusion.134
  174.1 1.0 fusion.133
  175.2 1.1 fusion.134
  178.3 1.0 fusion.133
  179.4 1.1 fusion.134
  182.5 1.0 fusion.133
  183.6 1.1 fusion.134
  185.5 2.1 %fusion.43 = bf16[1024,2,128]{2,0,1:T(8,128)(2,1)S(1)} fusion(f32[128,8,2,128]{3,2,0,1:T(2,128)} %bitcast.155, bf16[2,1024,128]{2,1,0:T(8,128)(2,1)} %get-tuple-element.223, bf16[128,128]{1,0:T(8,128)(2,1)S(1)} %copy-done.3), kind=kOutput, calls=%fused_computation.70 | convolution fusion | flops 67633152 | bytes 2129920 | tf_op jit(solution)/shard_map/dot_general | solution.py:96
  187.7 1.3 copy.49
  (239 shorter events, 27.0 us)
Async XLA Ops:
  0.0 21.0 %copy-start = (bf16[128,384]{1,0:T(8,128)(2,1)S(1)}, bf16[128,384]{1,0:T(8,128)(2,1)}, u32[]{:S(2)}) copy-start(bf16[128,384]{1,0:T(8,128)(2,1)} %param.19) | copy-start | bytes 294916
  0.9 10.1 %collective-permute-start = (bf16[1,256,128]{2,1,0:T(8,128)(2,1)S(1)}, bf16[1,256,128]{2,1,0:T(8,128)(2,1)S(1)}, u32[]{:S(2)}, u32[]{:S(2)}) collective-permute-start(bf16[1,256,128]{2,1,0:T(8,128)(2,1)S(1)} %get-tuple-element.356), channel_id=1, source_target_pairs={{0,4},{4,8},{8,12},{12,16},{16,20},{20,24},{24,28},{28,32},{32,36}... | collective-permute-start | bytes 196616 | tf_op jit(solution)/shard_map/ppermute | solution.py:16
  5.9 6.3 %collective-permute-start.1 = (bf16[1,256,128]{2,1,0:T(8,128)(2,1)S(1)}, bf16[1,256,128]{2,1,0:T(8,128)(2,1)S(1)}, u32[]{:S(2)}, u32[]{:S(2)}) collective-permute-start(bf16[1,256,128]{2,1,0:T(8,128)(2,1)S(1)} %get-tuple-element.355), channel_id=1, source_target_pairs={{4,0},{8,4},{12,8},{16,12},{20,16},{24,20},{28,24},{32,28},{36,32}... | collective-permute-start | bytes 196616 | tf_op jit(solution)/shard_map/ppermute | solution.py:19
  12.2 4.6 %collective-permute-start.2 = (bf16[10,1,128]{2,1,0:T(2,128)(2,1)S(1)}, bf16[10,1,128]{2,1,0:T(2,128)(2,1)S(1)}, u32[]{:S(2)}, u32[]{:S(2)}) collective-permute-start(bf16[10,1,128]{2,1,0:T(2,128)(2,1)S(1)} %get-tuple-element.353), channel_id=1, source_target_pairs={{0,1},{1,2},{2,3},{4,5},{5,6},{6,7},{8,9},{9,10},{10,11},{12,13},{... | collective-permute-start | bytes 7688 | tf_op jit(solution)/shard_map/ppermute | solution.py:16
  14.6 4.4 %collective-permute-start.3 = (bf16[10,1,128]{2,1,0:T(2,128)(2,1)S(1)}, bf16[10,1,128]{2,1,0:T(2,128)(2,1)S(1)}, u32[]{:S(2)}, u32[]{:S(2)}) collective-permute-start(bf16[10,1,128]{2,1,0:T(2,128)(2,1)S(1)} %get-tuple-element.354), channel_id=1, source_target_pairs={{1,0},{2,1},{3,2},{5,4},{6,5},{7,6},{9,8},{10,9},{11,10},{13,12},{... | collective-permute-start | bytes 7688 | tf_op jit(solution)/shard_map/ppermute | solution.py:19
  19.1 1.9 copy-start.6
  21.0 7.3 %copy-start.5 = (s32[16,16]{1,0:T(8,128)S(1)}, s32[16,16]{1,0:T(8,128)}, u32[]{:S(2)}) copy-start(s32[16,16]{1,0:T(8,128)} %param.17) | copy-start | bytes 3076
  22.1 6.7 %copy-start.1 = (bf16[8,256,384]{2,1,0:T(8,128)(2,1)}, bf16[8,256,384]{2,1,0:T(8,128)(2,1)S(1)}, u32[]{:S(2)}) copy-start(bf16[8,256,384]{2,1,0:T(8,128)(2,1)S(1)} %convolution_convert_fusion.1) | copy-start | bytes 4718596
  23.0 14.6 %collective-permute-start.4 = (bf16[8,128,256]{2,1,0:T(8,128)(2,1)}, bf16[8,128,256]{2,1,0:T(8,128)(2,1)}, u32[]{:S(2)}, u32[]{:S(2)}) collective-permute-start(bf16[8,128,256]{2,1,0:T(8,128)(2,1)} %get-tuple-element.351), channel_id=1, source_target_pairs={{0,1},{1,2},{2,3},{4,5},{5,6},{6,7},{8,9},{9,10},{10,11},{12,13},{... | collective-permute-start | bytes 1572872 | tf_op jit(solution)/shard_map/ppermute | solution.py:16
  26.9 15.4 %collective-permute-start.5 = (bf16[8,128,256]{2,1,0:T(8,128)(2,1)S(1)}, bf16[8,128,256]{2,1,0:T(8,128)(2,1)}, u32[]{:S(2)}, u32[]{:S(2)}) collective-permute-start(bf16[8,128,256]{2,1,0:T(8,128)(2,1)S(1)} %get-tuple-element.352), channel_id=1, source_target_pairs={{1,0},{2,1},{3,2},{5,4},{6,5},{7,6},{9,8},{10,9},{11,10},{13,12},{... | collective-permute-start | bytes 1572872 | tf_op jit(solution)/shard_map/ppermute | solution.py:19
  28.7 16.3 %slice-start = ((bf16[8,256,384]{2,1,0:T(8,128)(2,1)}), bf16[8,256,128]{2,1,0:T(8,128)(2,1)S(1)}, s32[]{:S(2)}) async-start(bf16[8,256,384]{2,1,0:T(8,128)(2,1)} %copy-done.1), calls=%async_computation.1 | async-start | bytes 1048576 | tf_op jit(solution)/shard_map/slice | solution.py:122
  45.1 29.7 %copy-start.4 = (bf16[128,128]{1,0:T(8,128)(2,1)S(1)}, bf16[128,128]{1,0:T(8,128)(2,1)}, u32[]{:S(2)}) copy-start(bf16[128,128]{1,0:T(8,128)(2,1)} %param.20) | copy-start | bytes 98308
  76.3 52.3 %all-to-all-start = ((bf16[8,256,128]{2,0,1:T(8,128)(2,1)}), bf16[8,256,128]{2,0,1:T(8,128)(2,1)S(1)}, u32[]{:S(2)}, u32[]{:S(2)}) async-start(bf16[8,256,128]{2,0,1:T(8,128)(2,1)} %copy.40), calls=%async_computation | async-start | bytes 1048576 | tf_op jit(solution)/shard_map/all_to_all | solution.py:153
  131.3 15.9 %copy-start.2 = (bf16[128,384]{1,0:T(8,128)(2,1)S(1)}, bf16[128,384]{1,0:T(8,128)(2,1)}, u32[]{:S(2)}) copy-start(bf16[128,384]{1,0:T(8,128)(2,1)} %param.22) | copy-start | bytes 294916
  131.3 15.9 %copy-start.7 = (f32[128]{0:T(128)S(1)}, f32[128]{0:T(128)}, u32[]{:S(2)}) copy-start(f32[128]{0:T(128)} %param.21) | copy-start | bytes 1540
  149.4 36.2 %copy-start.3 = (bf16[128,128]{1,0:T(8,128)(2,1)S(1)}, bf16[128,128]{1,0:T(8,128)(2,1)}, u32[]{:S(2)}) copy-start(bf16[128,128]{1,0:T(8,128)(2,1)} %param.23) | copy-start | bytes 98308
where the time goes:
time: 190 us; the launch traced here: 189 us
  waiting for transfers between devices  48.6 us (26%)
  matrix products  38.5 us (20%)
  starting transfers between devices  38 us (20%)
  local copies, waits for them, and re-layouts  30.4 us (16%)
  other arithmetic  26.6 us (14%)
  loops' own time  6.54 us (3%)
    all_to_all x1, waiting for transfers between devices, local(): lax.all_to_all(after_rows, 'slab', split_axis=1, concat_axis=0, tiled=True)  32.8 us
    all_to_all x1, starting transfers between devices, local(): lax.all_to_all(after_rows, 'slab', split_axis=1, concat_axis=0, tiled=True)  19.1 us
    dot_general x16, matrix products, attend(): jnp.einsum('hqk,khd->qhd', weights, value_heads, preferred_element_type=j...  16.9 us
    sub x16, matrix products, attend(): exp_terms = jnp.exp(scores - row_max)  15.5 us
    reduce_sum x2, other arithmetic, layer_norm(): spread = jnp.mean(centered * centered, axis=-1, keepdims=True)  15.4 us
    ppermute x3, starting transfers between devices, padded_2(): lax.ppermute(lax.slice_in_dim(block, block.shape[dim] - width, None, axis...  11.2 us
    dynamic_slice x32, local copies, waits for them, and re-layouts, local(): mixture = lax.map(row_attend, (queries, kv_wide, query_ok, key_ok))  9.88 us
    ppermute x3, waiting for transfers between devices, padded_2(): lax.ppermute(lax.slice_in_dim(block, block.shape[dim] - width, None, axis...  8.91 us
  transfers between devices with their start and end apart: 7, of which 4 were waited for; matrix products, arithmetic and copies ran while one was open for 1% of the time, Pallas kernels for 0%

commit v1 on v0

--- a/solution.py
+++ b/solution.py
@@ -3,6 +3,7 @@
 import jax.numpy as jnp
 from jax import lax
 from jax.sharding import PartitionSpec as P
+from jax.lax import all_to_all, axis_size
 
 HEAD_DIM = 32
 COL_REACH = 128
@@ -150,7 +151,8 @@
     after_rows = (
         stream.astype(jnp.float32) + jnp.dot(mixture, row_out, preferred_element_type=jnp.float32)
     ).astype(jnp.bfloat16)
-    columns = lax.all_to_all(after_rows, "slab", split_axis=1, concat_axis=0, tiled=True)
+    current_arr = jnp.stack(jnp.split(after_rows, axis_size("slab"), axis=1))
+    columns = jnp.concatenate(all_to_all(current_arr, "slab", 0, 0), axis=0)
     col_ids = (
         tile_at * length + slab_at * col_count + jnp.arange(col_count, dtype=jnp.int32)
     ) // block_size

time: 190 us -> 252 us (1.33)
  local copies, waits for them, and re-layouts: 30.4 us -> 103 us
  other arithmetic: 26.6 us -> 18.5 us
    unnamed x18 -> x147, local copies, waits for them, and re-layouts: 1.16 us -> 77.4 us
    reduce_sum x2, other arithmetic: 15.4 us -> 3.36 us  [layer_norm(): spread = jnp.mean(centered * centered, axis=-1, keepdims=True)]
where the time goes in v1:
time: 252 us
  local copies, waits for them, and re-layouts  103 us (41%)
  waiting for transfers between devices  48.6 us (19%)
  starting transfers between devices  38 us (15%)
  matrix products  36.2 us (14%)
  other arithmetic  18.5 us (7%)
  loops' own time  6.95 us (3%)
    unnamed x147, local copies, waits for them, and re-layouts  77.4 us
    all_to_all x1, waiting for transfers between devices, local(): columns = jnp.concatenate(all_to_all(current_arr, 'slab', 0, 0), axis=0)  32.8 us
    all_to_all x1, starting transfers between devices, local(): columns = jnp.concatenate(all_to_all(current_arr, 'slab', 0, 0), axis=0)  19.1 us
    dot_general x16, matrix products, attend(): jnp.einsum('hqk,khd->qhd', weights, value_heads, preferred_element_type=j...  17 us
    sub x16, matrix products, attend(): exp_terms = jnp.exp(scores - row_max)  15.5 us
    ppermute x3, starting transfers between devices, padded_2(): lax.ppermute(lax.slice_in_dim(block, block.shape[dim] - width, None, axis...  11.2 us
    dynamic_slice x32, local copies, waits for them, and re-layouts, local(): mixture = lax.map(row_attend, (queries, kv_wide, query_ok, key_ok))  9.88 us
    ppermute x3, waiting for transfers between devices, padded_2(): lax.ppermute(lax.slice_in_dim(block, block.shape[dim] - width, None, axis...  8.91 us
  transfers between devices with their start and end apart: 7, of which 4 were waited for; matrix products, arithmetic and copies ran while one was open for 1% of the time, Pallas kernels for 0%

profile of v1, /device:TPU:1, one launch (start us, length us, event | category | flops | bytes accessed | tf_op | source)
XLA Modules:
  0.0 251.6 jit_solution(4308076617421250878)
XLA Ops:
  0.9 4.9 %collective-permute-start = (bf16[1,256,128]{2,1,0:T(8,128)(2,1)S(1)}, bf16[1,256,128]{2,1,0:T(8,128)(2,1)S(1)}, u32[]{:S(2)}, u32[]{:S(2)}) collective-permute-start(bf16[1,256,128]{2,1,0:T(8,128)(2,1)S(1)} %get-tuple-element.326), channel_id=1, source_target_pairs={{0,4},{4,8},{8,12},{12,16},{16,20},{20,24},{24,28},{28,32},{32,36}... | collective-permute-start | bytes 196616 | tf_op jit(solution)/shard_map/ppermute | solution.py:17
  5.9 5.1 %collective-permute-start.1 = (bf16[1,256,128]{2,1,0:T(8,128)(2,1)S(1)}, bf16[1,256,128]{2,1,0:T(8,128)(2,1)S(1)}, u32[]{:S(2)}, u32[]{:S(2)}) collective-permute-start(bf16[1,256,128]{2,1,0:T(8,128)(2,1)S(1)} %get-tuple-element.325), channel_id=1, source_target_pairs={{4,0},{8,4},{12,8},{16,12},{20,16},{24,20},{28,24},{32,28},{36,32}... | collective-permute-start | bytes 196616 | tf_op jit(solution)/shard_map/ppermute | solution.py:20
  11.0 1.1 constant_dynamic-update-slice_fusion.3
  12.2 2.4 collective-permute-start.2
  14.6 1.3 collective-permute-start.3
  16.8 2.2 collective-permute-done.3
  19.1 1.2 convert_reduce_fusion
  21.0 1.0 convolution_convert_fusion.1
  22.1 1.0 fusion.77
  23.0 3.9 %collective-permute-start.4 = (bf16[8,128,256]{2,1,0:T(8,128)(2,1)}, bf16[8,128,256]{2,1,0:T(8,128)(2,1)}, u32[]{:S(2)}, u32[]{:S(2)}) collective-permute-start(bf16[8,128,256]{2,1,0:T(8,128)(2,1)} %get-tuple-element.319), channel_id=1, source_target_pairs={{0,1},{1,2},{2,3},{4,5},{5,6},{6,7},{8,9},{9,10},{10,11},{12,13},{... | collective-permute-start | bytes 1572872 | tf_op jit(solution)/shard_map/ppermute | solution.py:17
  26.9 1.3 collective-permute-start.5
  28.8 8.9 %collective-permute-done.4 = bf16[8,128,256]{2,1,0:T(8,128)(2,1)} collective-permute-done((bf16[8,128,256]{2,1,0:T(8,128)(2,1)}, bf16[8,128,256]{2,1,0:T(8,128)(2,1)}, u32[]{:S(2)}, u32[]{:S(2)}) %collective-permute-start.4) | collective-permute-done | bytes 524320 | tf_op jit(solution)/shard_map/ppermute | solution.py:17
  37.7 4.7 %collective-permute-done.5 = bf16[8,128,256]{2,1,0:T(8,128)(2,1)} collective-permute-done((bf16[8,128,256]{2,1,0:T(8,128)(2,1)S(1)}, bf16[8,128,256]{2,1,0:T(8,128)(2,1)}, u32[]{:S(2)}, u32[]{:S(2)}) %collective-permute-start.5) | collective-permute-done | bytes 524320 | tf_op jit(solution)/shard_map/ppermute | solution.py:20
  42.4 2.7 %pad_maximum_fusion = bf16[8,512,256]{2,1,0:T(8,128)(2,1)} fusion(bf16[8,128,256]{2,1,0:T(8,128)(2,1)} %collective-permute-done.5, bf16[8,256,256]{2,1,0:T(8,128)(2,1)S(1)} %slice.161, bf16[8,128,256]{2,1,0:T(8,128)(2,1)} %collective-permute-done.4), kind=kLoop, calls=%fused_computation.61 | loop fusion | flops 6291456 | bytes 4194304 | tf_op jit(solution)/shard_map/concatenate | solution.py:21
  45.1 29.7 %while.45 = (s32[]{:T(128)}, bf16[8,256,128]{1,2,0:T(8,128)(2,1)S(1)}, bf16[8,512,256]{2,1,0:T(8,128)(2,1)}, s32[8,512]{1,0:T(8,128)S(1)}, bf16[8,256,128]{2,1,0...) while((s32[]{:T(128)}, bf16[8,256,128]{1,2,0:T(8,128)(2,1)S(1)}, ...), condition=%wide.region_5.6_spmd.clone, body=%wide.region_2.5_spmd.clone.sunk | while | flops 106237440 | bytes 2969721 | solution.py:150
  45.4 1.0 constant_dynamic-slice_fusion.12
  46.7 1.0 fusion.118
  47.7 1.1 fusion.120
  49.1 1.0 constant_dynamic-slice_fusion.12
  50.4 1.0 fusion.118
  51.4 1.1 fusion.120
  52.8 1.0 constant_dynamic-slice_fusion.12
  54.1 1.0 fusion.118
  55.1 1.1 fusion.120
  56.5 1.0 constant_dynamic-slice_fusion.12
  57.8 1.0 fusion.118
  58.8 1.1 fusion.120
  60.2 1.0 constant_dynamic-slice_fusion.12
  61.5 1.0 fusion.118
  62.5 1.1 fusion.120
  64.0 1.0 constant_dynamic-slice_fusion.12
  65.2 1.0 fusion.118
  66.2 1.1 fusion.120
  67.7 1.0 constant_dynamic-slice_fusion.12
  69.0 1.0 fusion.118
  69.9 1.1 fusion.120
  71.4 1.0 constant_dynamic-slice_fusion.12
  72.7 1.0 fusion.118
  73.7 1.1 fusion.120
  152.0 19.1 %all-to-all-start = ((bf16[128,8,2,128]{3,2,1,0:T(2,128)(2,1)}), bf16[128,8,2,128]{3,2,1,0:T(2,128)(2,1)S(1)}, u32[]{:S(2)}, u32[]{:S(2)}) async-start(bf16[128,8,2,128]{3,2,1,0:T(2,128)(2,1)} %constant_dynamic-update-slice_fusion.5), calls=%async_computation | async-start | bytes 1048576 | tf_op jit(solution)/shard_map/all_to_all | solution.py:155
  171.5 32.8 %all-to-all-done = bf16[128,8,2,128]{3,2,1,0:T(2,128)(2,1)S(1)} async-done(((bf16[128,8,2,128]{3,2,1,0:T(2,128)(2,1)}), bf16[128,8,2,128]{3,2,1,0:T(2,128)(2,1)S(1)}, u32[]{:S(2)}, u32[]{:S(2)}) %all-to-all-start) | async-done | bytes 524320 | tf_op jit(solution)/shard_map/all_to_all | solution.py:155
  204.3 1.2 convert_reduce_fusion.1
  205.5 2.7 %multiply_reduce_fusion = f32[128,8,2]{2,1,0:T(8,128)S(1)} fusion(bf16[128,8,2,128]{3,2,1,0:T(2,128)(2,1)S(1)} %all-to-all-done, f32[128,8,2]{2,1,0:T(8,128)S(1)} %get-tuple-element.324), kind=kLoop, calls=%fused_computation.96 | loop fusion | flops 1046528 | bytes 540672 | tf_op jit(solution)/shard_map/reduce_sum | solution.py:84
  208.4 2.5 multiply_convert_fusion
  211.5 36.1 %while.44 = (s32[]{:T(128)}, bf16[2,1024,128]{2,1,0:T(8,128)(2,1)}, bf16[2,1024,384]{1,2,0:T(8,128)(2,1)S(1)}, s32[2,1024]{1,0:T(2,128)S(1)}, s32[]{:T(128)}, /*...) while((s32[]{:T(128)}, bf16[2,1024,128]{2,1,0:T(8,128)(2,1)}, ...), condition=%wide.region_13.14_spmd, body=%wide.region_8.13_spmd.sunk | while | flops 106237968 | bytes 6797429 | solution.py:93
  211.8 17.0 %while.46 = (s32[]{:T(128)}, bf16[4,256,128]{2,1,0:T(8,128)(2,1)S(1)}, s32[4]{0:T(128)S(1)}, bf16[1280,256]{0,1:T(8,128)(2,1)S(1)}, s32[1280]{0:T(1024)S(1)}, /*...) while((s32[]{:T(128)}, ...), condition=%wide.region_12.12_spmd.clone, body=%wide.region_9.11_spmd.clone.sunk | while | flops 106236688 | bytes 1924418 | solution.py:76
  213.7 1.0 fusion.127
  214.8 1.1 fusion.128
  219.1 1.1 fusion.128
  222.3 1.0 fusion.127
  223.3 1.1 fusion.128
  226.5 1.0 fusion.127
  227.6 1.1 fusion.128
  229.8 17.0 %while.46 = (s32[]{:T(128)}, bf16[4,256,128]{2,1,0:T(8,128)(2,1)S(1)}, s32[4]{0:T(128)S(1)}, bf16[1280,256]{0,1:T(8,128)(2,1)S(1)}, s32[1280]{0:T(1024)S(1)}, /*...) while((s32[]{:T(128)}, ...), condition=%wide.region_12.12_spmd.clone, body=%wide.region_9.11_spmd.clone.sunk | while | flops 106236688 | bytes 1924418 | solution.py:76
  231.8 1.0 fusion.127
  232.8 1.1 fusion.128
  237.1 1.1 fusion.128
  240.3 1.0 fusion.127
  241.3 1.1 fusion.128
  244.5 1.0 fusion.127
  245.6 1.1 fusion.128
  247.6 1.4 bitcast_convert_fusion
  249.0 1.3 fusion.43
  250.3 1.3 copy.15
  (359 shorter events, 101.9 us)
Async XLA Ops:
  0.0 21.0 %copy-start = (bf16[128,384]{1,0:T(8,128)(2,1)S(1)}, bf16[128,384]{1,0:T(8,128)(2,1)}, u32[]{:S(2)}) copy-start(bf16[128,384]{1,0:T(8,128)(2,1)} %param.19) | copy-start | bytes 294916
  0.9 10.1 %collective-permute-start = (bf16[1,256,128]{2,1,0:T(8,128)(2,1)S(1)}, bf16[1,256,128]{2,1,0:T(8,128)(2,1)S(1)}, u32[]{:S(2)}, u32[]{:S(2)}) collective-permute-start(bf16[1,256,128]{2,1,0:T(8,128)(2,1)S(1)} %get-tuple-element.326), channel_id=1, source_target_pairs={{0,4},{4,8},{8,12},{12,16},{16,20},{20,24},{24,28},{28,32},{32,36}... | collective-permute-start | bytes 196616 | tf_op jit(solution)/shard_map/ppermute | solution.py:17
  5.9 6.3 %collective-permute-start.1 = (bf16[1,256,128]{2,1,0:T(8,128)(2,1)S(1)}, bf16[1,256,128]{2,1,0:T(8,128)(2,1)S(1)}, u32[]{:S(2)}, u32[]{:S(2)}) collective-permute-start(bf16[1,256,128]{2,1,0:T(8,128)(2,1)S(1)} %get-tuple-element.325), channel_id=1, source_target_pairs={{4,0},{8,4},{12,8},{16,12},{20,16},{24,20},{28,24},{32,28},{36,32}... | collective-permute-start | bytes 196616 | tf_op jit(solution)/shard_map/ppermute | solution.py:20
  12.2 4.6 %collective-permute-start.2 = (bf16[10,1,128]{2,1,0:T(2,128)(2,1)S(1)}, bf16[10,1,128]{2,1,0:T(2,128)(2,1)S(1)}, u32[]{:S(2)}, u32[]{:S(2)}) collective-permute-start(bf16[10,1,128]{2,1,0:T(2,128)(2,1)S(1)} %get-tuple-element.321), channel_id=1, source_target_pairs={{0,1},{1,2},{2,3},{4,5},{5,6},{6,7},{8,9},{9,10},{10,11},{12,13},{... | collective-permute-start | bytes 7688 | tf_op jit(solution)/shard_map/ppermute | solution.py:17
  14.6 4.4 %collective-permute-start.3 = (bf16[10,1,128]{2,1,0:T(2,128)(2,1)S(1)}, bf16[10,1,128]{2,1,0:T(2,128)(2,1)S(1)}, u32[]{:S(2)}, u32[]{:S(2)}) collective-permute-start(bf16[10,1,128]{2,1,0:T(2,128)(2,1)S(1)} %get-tuple-element.322), channel_id=1, source_target_pairs={{1,0},{2,1},{3,2},{5,4},{6,5},{7,6},{9,8},{10,9},{11,10},{13,12},{... | collective-permute-start | bytes 7688 | tf_op jit(solution)/shard_map/ppermute | solution.py:20
  19.1 1.9 copy-start.7
  21.0 7.3 %copy-start.6 = (s32[16,16]{1,0:T(8,128)S(1)}, s32[16,16]{1,0:T(8,128)}, u32[]{:S(2)}) copy-start(s32[16,16]{1,0:T(8,128)} %param.17) | copy-start | bytes 3076
  22.1 6.7 %copy-start.2 = (bf16[8,256,384]{2,1,0:T(8,128)(2,1)}, bf16[8,256,384]{2,1,0:T(8,128)(2,1)S(1)}, u32[]{:S(2)}) copy-start(bf16[8,256,384]{2,1,0:T(8,128)(2,1)S(1)} %convolution_convert_fusion.1) | copy-start | bytes 4718596
  23.0 14.6 %collective-permute-start.4 = (bf16[8,128,256]{2,1,0:T(8,128)(2,1)}, bf16[8,128,256]{2,1,0:T(8,128)(2,1)}, u32[]{:S(2)}, u32[]{:S(2)}) collective-permute-start(bf16[8,128,256]{2,1,0:T(8,128)(2,1)} %get-tuple-element.319), channel_id=1, source_target_pairs={{0,1},{1,2},{2,3},{4,5},{5,6},{6,7},{8,9},{9,10},{10,11},{12,13},{... | collective-permute-start | bytes 1572872 | tf_op jit(solution)/shard_map/ppermute | solution.py:17
  26.9 15.4 %collective-permute-start.5 = (bf16[8,128,256]{2,1,0:T(8,128)(2,1)S(1)}, bf16[8,128,256]{2,1,0:T(8,128)(2,1)}, u32[]{:S(2)}, u32[]{:S(2)}) collective-permute-start(bf16[8,128,256]{2,1,0:T(8,128)(2,1)S(1)} %get-tuple-element.320), channel_id=1, source_target_pairs={{1,0},{2,1},{3,2},{5,4},{6,5},{7,6},{9,8},{10,9},{11,10},{13,12},{... | collective-permute-start | bytes 1572872 | tf_op jit(solution)/shard_map/ppermute | solution.py:20
  28.7 16.3 %slice-start = ((bf16[8,256,384]{2,1,0:T(8,128)(2,1)}), bf16[8,256,128]{2,1,0:T(8,128)(2,1)S(1)}, s32[]{:S(2)}) async-start(bf16[8,256,384]{2,1,0:T(8,128)(2,1)} %copy-done.2), calls=%async_computation.1 | async-start | bytes 1048576 | tf_op jit(solution)/shard_map/slice | solution.py:123
  45.1 29.7 %copy-start.5 = (bf16[128,128]{1,0:T(8,128)(2,1)S(1)}, bf16[128,128]{1,0:T(8,128)(2,1)}, u32[]{:S(2)}) copy-start(bf16[128,128]{1,0:T(8,128)(2,1)} %param.20) | copy-start | bytes 98308
  152.0 52.3 %all-to-all-start = ((bf16[128,8,2,128]{3,2,1,0:T(2,128)(2,1)}), bf16[128,8,2,128]{3,2,1,0:T(2,128)(2,1)S(1)}, u32[]{:S(2)}, u32[]{:S(2)}) async-start(bf16[128,8,2,128]{3,2,1,0:T(2,128)(2,1)} %constant_dynamic-update-slice_fusion.5), calls=%async_computation | async-start | bytes 1048576 | tf_op jit(solution)/shard_map/all_to_all | solution.py:155
  204.3 4.1 %copy-start.1 = (bf16[128,8,2,128]{3,2,1,0:T(2,128)(2,1)}, bf16[128,8,2,128]{3,2,1,0:T(2,128)(2,1)S(1)}, u32[]{:S(2)}) copy-start(bf16[128,8,2,128]{3,2,1,0:T(2,128)(2,1)S(1)} %all-to-all-done) | copy-start | bytes 1572868
  205.4 2.9 %copy-start.8 = (f32[128]{0:T(128)S(1)}, f32[128]{0:T(128)}, u32[]{:S(2)}) copy-start(f32[128]{0:T(128)} %param.21) | copy-start | bytes 1540
  205.5 5.3 %copy-start.3 = (bf16[128,384]{1,0:T(8,128)(2,1)S(1)}, bf16[128,384]{1,0:T(8,128)(2,1)}, u32[]{:S(2)}) copy-start(bf16[128,384]{1,0:T(8,128)(2,1)} %param.22) | copy-start | bytes 294916
  211.5 37.5 %copy-start.4 = (bf16[128,128]{1,0:T(8,128)(2,1)S(1)}, bf16[128,128]{1,0:T(8,128)(2,1)}, u32[]{:S(2)}) copy-start(bf16[128,128]{1,0:T(8,128)(2,1)} %param.23) | copy-start | bytes 98308
